TPU v7x, 256 devices: a whole 4x4x8 slice. The times are simulated.
256 devices in a mesh: strike: 64 (over z, y_hi, x), dip: 4 (over y_lo, core).
Axes of the slice: x: 4, y: 4 (y_hi: 2, y_lo: 2; y = y_hi * 2 + y_lo), z: 8, core: 2. Of those that a mesh axis runs over, the one named last changes fastest.
Arguments:
- coarse_field: bfloat16 [256, 16, 128], P('strike', 'dip'), may hold values from -6 to 6
- up_weight: bfloat16 [8, 8, 8, 32, 32], replicated, may hold values from -0.375 to 0.375
- first_weight: bfloat16 [3, 3, 3, 32, 32], replicated, may hold values from -0.21875 to 0.21875
- second_weight: bfloat16 [3, 3, 3, 32, 32], replicated, may hold values from -0.21875 to 0.21875
Outputs:
- refined: bfloat16 [1024, 64, 512], P('strike', 'dip')
All inputs are finite; a program needn't handle non-finite values.
Results may differ from a plain program's by a relative error of at most 0.012.
Values may be sent and summed in bfloat16 or wider, within the bound.
A program may use at most 192 MiB of HBM per device.

v0:
```python
import jax
import jax.numpy as jnp
import numpy as np
from jax import lax
from jax.sharding import PartitionSpec as P

HIGHEST = lax.Precision.HIGHEST


def passed_along(block, axis, distance):
    devices = range(lax.axis_size(axis))
    route = [(i - distance, i) for i in devices if i - distance in devices]
    return lax.ppermute(block, axis, route)


def extended_2(cells, sides, width):
    for axis, dim in sides:
        count = lax.axis_size(axis)
        ends = count - 1
        head = lax.slice_in_dim(cells, 0, width, axis=dim)
        tail = lax.slice_in_dim(cells, cells.shape[dim] - width, cells.shape[dim], axis=dim)
        cells = jnp.concatenate(
            [
                lax.ppermute(tail, axis, [(i, (i + 1) % count) for i in range(ends)]),
                cells,
                lax.ppermute(head, axis, [((i + 1) % count, i) for i in range(ends)]),
            ],
            axis=dim,
        )
    return cells


def up_tables(up_weight, coarse_depth):
    channels = up_weight.shape[3]
    fine_depth = 4 * coarse_depth
    coarse_pos = np.arange(coarse_depth)[:, None, None]
    kernel_pos = np.arange(8)[None, :, None]
    fine_pos = np.arange(fine_depth)[None, None, :]
    tap_table = (4 * coarse_pos + kernel_pos - 2 == fine_pos).astype(np.float32)
    placed = jnp.einsum(
        "akf,ijkcd->ijacfd",
        jnp.asarray(tap_table),
        up_weight.astype(jnp.float32),
        precision=HIGHEST,
    )
    placed = placed.reshape(2, 4, 2, 4, coarse_depth * channels, fine_depth * channels)
    placed = placed.transpose(0, 2, 4, 1, 3, 5)
    return placed.reshape(2, 2, coarse_depth * channels, 16 * fine_depth * channels).astype(
        jnp.bfloat16
    )


def band_tables(weight):
    channels = weight.shape[3]
    cells_in = np.array([0, 1, 2, 3, -1, 4])
    tap_table = (
        cells_in[:, None, None] == np.arange(4)[None, None, :] + np.arange(3)[None, :, None] - 1
    )
    band_mats = jnp.einsum(
        "rdo,xydce->xyrcoe",
        jnp.asarray(tap_table.astype(np.float32)),
        weight.astype(jnp.float32),
        precision=HIGHEST,
    )
    return band_mats.reshape(3, 3, 6 * channels, 4 * channels).astype(jnp.bfloat16)


def spread(coarse_block, up_mats):
    size_one, size_two, depth_lanes = coarse_block.shape
    lane_width = up_mats.shape[3] // 16
    flat_rows = coarse_block.reshape(size_one * size_two, depth_lanes)
    summed = jnp.zeros((size_one + 1, size_two + 1, 4, 4, lane_width), jnp.float32)
    for high_one in (0, 1):
        for high_two in (0, 1):
            product = jnp.dot(
                flat_rows, up_mats[high_one, high_two], preferred_element_type=jnp.float32
            )
            product = product.reshape(size_one, size_two, 4, 4, lane_width)
            summed = summed + jnp.pad(
                product,
                ((high_one, 1 - high_one), (high_two, 1 - high_two), (0, 0), (0, 0), (0, 0)),
            )
    summed = summed.transpose(0, 2, 1, 3, 4)
    return summed.reshape(4 * size_one + 4, 4 * size_two + 4, lane_width)


def refine(padded, band_mats, rows_out, cols_out):
    size_one, size_two, depth_lanes = padded.shape
    quad_lanes = band_mats.shape[3]
    channels = quad_lanes // 4
    groups = depth_lanes // quad_lanes
    blocks = padded.reshape(size_one, size_two, groups, quad_lanes)
    before_cell = jnp.pad(blocks[:, :, :-1, 3 * channels :], ((0, 0), (0, 0), (1, 0), (0, 0)))
    after_cell = jnp.pad(blocks[:, :, 1:, :channels], ((0, 0), (0, 0), (0, 1), (0, 0)))
    widened = jnp.concatenate([blocks, before_cell, after_cell], axis=3)
    summed = jnp.zeros((rows_out * cols_out * groups, quad_lanes), jnp.float32)
    for shift_one in range(3):
        for shift_two in range(3):
            window = widened[shift_one : shift_one + rows_out, shift_two : shift_two + cols_out]
            summed = summed + jnp.dot(
                window.reshape(-1, 6 * channels),
                band_mats[shift_one, shift_two],
                preferred_element_type=jnp.float32,
            )
    return summed.reshape(rows_out, cols_out, depth_lanes)


def strike_move(edge_rows, step):
    return passed_along(edge_rows, "strike", step)


def dip_move(edge_cols, step):
    return passed_along(edge_cols.astype(jnp.bfloat16), "dip", step).astype(edge_cols.dtype)


def conv_step(field_in, band_mats):
    padded = extended_2(field_in, (("strike", 0), ("dip", 1)), 1)
    return refine(padded, band_mats, field_in.shape[0], field_in.shape[1])


def body(coarse_field, up_weight, first_weight, second_weight):
    channels = up_weight.shape[3]
    coarse_depth = coarse_field.shape[2] // channels
    up_mats = up_tables(up_weight, coarse_depth)
    own_rows = 4 * coarse_field.shape[0]
    own_cols = 4 * coarse_field.shape[1]
    first_mats = band_tables(first_weight)
    second_mats = band_tables(second_weight)
    extended = spread(coarse_field, up_mats)
    from_below = strike_move(extended[own_rows + 2 :], 1)
    from_above = strike_move(extended[:2], -1)
    strip = extended[2 : own_rows + 2].at[:2].add(from_below).at[own_rows - 2 :].add(from_above)
    from_left = dip_move(strip[:, own_cols + 2 :], 1)
    from_right = dip_move(strip[:, :2], -1)
    summed = (
        strip[:, 2 : own_cols + 2].at[:, :2].add(from_left).at[:, own_cols - 2 :].add(from_right)
    )
    base = jax.nn.silu(summed).astype(jnp.bfloat16)
    hidden = jax.nn.silu(conv_step(base, first_mats)).astype(jnp.bfloat16)
    second_out = conv_step(hidden, second_mats)
    return (base.astype(jnp.float32) + second_out).astype(jnp.bfloat16)


def solution(mesh):
    return jax.shard_map(
        body,
        mesh=mesh,
        in_specs=(P("strike", "dip", None), P(), P(), P()),
        out_specs=P("strike", "dip", None),
        check_vma=False,
    )
```

profile of v0, /device:TPU:126, one launch (start us, length us, event | category | flops | bytes accessed | tf_op | source)
XLA Modules:
  0.0 237.9 jit_solution(1017128933917467765)
XLA Ops:
  0.0 30.9 %convert_bitcast_fusion = bf16[8,8,4,32,16,32]{5,4,3,1,0,2:T(8,128)(2,1)} fusion(f32[4,8,16,1,1,1]{2,1,5,4,3,0:T(8,128)} %constant.138, bf16[8,8,8,32,32]{4,3,2,1,0:T(8,128)(2,1)} %param.16), kind=kOutput, calls=%fused_computation | convolution fusion | flops 406847488 | bytes 9439232 | tf_op jit(solution)/shard_map/akf,ijkcd->ijacfd/dot_general | solution.py:40
  30.9 22.9 %copy.13 = bf16[8,8,4,32,16,32]{5,4,3,2,1,0:T(8,128)(2,1)} copy(bf16[8,8,4,32,16,32]{5,4,3,1,0,2:T(8,128)(2,1)} %convert_bitcast_fusion) | data formatting | bytes 16777216 | tf_op jit(solution)/shard_map/convert_element_type | solution.py:48
  53.8 43.7 %convert_element_type.72 = bf16[2,4,2,4,128,512]{5,4,3,2,1,0:T(8,128)(2,1)} reshape(bf16[8,8,4,32,16,32]{5,4,3,2,1,0:T(8,128)(2,1)} %copy.13) | data formatting | bytes 16777216 | tf_op jit(solution)/shard_map/convert_element_type | solution.py:48
  97.5 13.2 %copy.14 = bf16[2,2,128,4,4,512]{2,5,4,3,1,0:T(8,128)(2,1)} copy(bf16[2,2,128,4,4,512]{5,2,4,1,3,0:T(8,128)(2,1)} %bitcast.135) | data formatting | bytes 16777216 | tf_op jit(solution)/shard_map/convert_element_type | solution.py:48
  110.8 2.2 convolution_bitcast_fusion.3
  113.0 2.3 convolution_bitcast_fusion.2
  115.3 2.3 convolution_bitcast_fusion.1
  117.5 2.3 convolution_bitcast_fusion
  121.9 5.6 %collective-permute-start = (f32[2,20,512]{2,1,0:T(8,128)S(1)}, f32[2,20,512]{2,1,0:T(8,128)S(1)}, u32[]{:S(2)}, u32[]{:S(2)}) collective-permute-start(f32[2,20,512]{2,1,0:T(8,128)S(1)} %get-tuple-element.54), channel_id=1, source_target_pairs={{0,4},{4,8},{8,12},{12,16},{16,20},{20,24},{24,28},{28,32},{32,36}... | collective-permute-start | bytes 245768 | tf_op jit(solution)/shard_map/ppermute | solution.py:13
  127.5 1.9 collective-permute-start.1
  129.8 10.0 %collective-permute-done.1 = f32[2,20,512]{2,1,0:T(8,128)S(1)} collective-permute-done((f32[2,20,512]{2,1,0:T(8,128)S(1)}, f32[2,20,512]{2,1,0:T(8,128)S(1)}, u32[]{:S(2)}, u32[]{:S(2)}) %collective-permute-start.1) | collective-permute-done | bytes 81952 | tf_op jit(solution)/shard_map/ppermute | solution.py:13
  139.9 1.9 collective-permute-start.2
  141.9 3.6 %collective-permute-start.3 = (bf16[16,2,512]{2,1,0:T(2,128)(2,1)S(1)}, bf16[16,2,512]{2,1,0:T(2,128)(2,1)S(1)}, u32[]{:S(2)}, u32[]{:S(2)}) collective-permute-start(bf16[16,2,512]{2,1,0:T(2,128)(2,1)S(1)} %get-tuple-element.73), channel_id=1, source_target_pairs={{1,0},{2,1},{3,2},{5,4},{6,5},{7,6},{9,8},{10,9},{11,10},{13,12},{... | collective-permute-start | bytes 98312 | tf_op jit(solution)/shard_map/ppermute | solution.py:13
  147.4 1.9 collective-permute-start.4
  149.3 3.9 %collective-permute-start.5 = (bf16[1,16,512]{2,1,0:T(8,128)(2,1)S(1)}, bf16[1,16,512]{2,1,0:T(8,128)(2,1)S(1)}, u32[]{:S(2)}, u32[]{:S(2)}) collective-permute-start(bf16[1,16,512]{2,1,0:T(8,128)(2,1)S(1)} %get-tuple-element.86), channel_id=1, source_target_pairs={{4,0},{8,4},{12,8},{16,12},{20,16},{24,20},{28,24},{32,28},{36,32}... | collective-permute-start | bytes 49160 | tf_op jit(solution)/shard_map/ppermute | solution.py:26
  153.3 7.4 %collective-permute-done.5 = bf16[1,16,512]{2,1,0:T(8,128)(2,1)S(1)} collective-permute-done((bf16[1,16,512]{2,1,0:T(8,128)(2,1)S(1)}, bf16[1,16,512]{2,1,0:T(8,128)(2,1)S(1)}, u32[]{:S(2)}, u32[]{:S(2)}) %collective-permute-start.5) | collective-permute-done | bytes 16416 | tf_op jit(solution)/shard_map/ppermute | solution.py:26
  160.7 1.9 collective-permute-start.6
  162.7 3.8 %collective-permute-start.7 = (bf16[18,1,512]{2,1,0:T(2,128)(2,1)S(1)}, bf16[18,1,512]{2,1,0:T(2,128)(2,1)S(1)}, u32[]{:S(2)}, u32[]{:S(2)}) collective-permute-start(bf16[18,1,512]{2,1,0:T(2,128)(2,1)S(1)} %get-tuple-element.82), channel_id=1, source_target_pairs={{1,0},{2,1},{3,2},{5,4},{6,5},{7,6},{9,8},{10,9},{11,10},{13,12},{... | collective-permute-start | bytes 55304 | tf_op jit(solution)/shard_map/ppermute | solution.py:26
  166.5 2.3 convert_bitcast_fusion.2
  173.4 3.4 %fusion.19 = (bf16[16,16,4,192]{3,2,1,0:T(4,128)(2,1)}, bf16[16,16,4,192]{3,2,1,0:T(4,128)(2,1)S(1)}, bf16[16,16,4,192]{3,2,1,0:T(4,128)(2,1)S(1)}, bf16[16,16,4...) fusion(bf16[18,18,4,192]{3,2,1,0:T(4,128)(2,1)S(1)} %fusion.5), kind=kLoop, calls=%fused_computation.85 | loop fusion | bytes 7077888 | tf_op jit(solution)/shard_map/slice | solution.py:99
  176.8 2.2 reshape.216
  179.0 2.2 reshape.217
  181.2 2.2 reshape.218
  192.3 1.9 collective-permute-start.8
  194.2 3.9 %collective-permute-start.9 = (bf16[1,16,512]{2,1,0:T(8,128)(2,1)S(1)}, bf16[1,16,512]{2,1,0:T(8,128)(2,1)S(1)}, u32[]{:S(2)}, u32[]{:S(2)}) collective-permute-start(bf16[1,16,512]{2,1,0:T(8,128)(2,1)S(1)} %get-tuple-element.84), channel_id=1, source_target_pairs={{4,0},{8,4},{12,8},{16,12},{20,16},{24,20},{28,24},{32,28},{36,32}... | collective-permute-start | bytes 49160 | tf_op jit(solution)/shard_map/ppermute | solution.py:26
  198.1 7.4 %collective-permute-done.9 = bf16[1,16,512]{2,1,0:T(8,128)(2,1)S(1)} collective-permute-done((bf16[1,16,512]{2,1,0:T(8,128)(2,1)S(1)}, bf16[1,16,512]{2,1,0:T(8,128)(2,1)S(1)}, u32[]{:S(2)}, u32[]{:S(2)}) %collective-permute-start.9) | collective-permute-done | bytes 16416 | tf_op jit(solution)/shard_map/ppermute | solution.py:26
  207.5 3.9 %collective-permute-start.11 = (bf16[18,1,512]{2,1,0:T(2,128)(2,1)S(1)}, bf16[18,1,512]{2,1,0:T(2,128)(2,1)S(1)}, u32[]{:S(2)}, u32[]{:S(2)}) collective-permute-start(bf16[18,1,512]{2,1,0:T(2,128)(2,1)S(1)} %get-tuple-element.80), channel_id=1, source_target_pairs={{1,0},{2,1},{3,2},{5,4},{6,5},{7,6},{9,8},{10,9},{11,10},{13,12},{... | collective-permute-start | bytes 55304 | tf_op jit(solution)/shard_map/ppermute | solution.py:26
  211.4 2.3 convert_bitcast_fusion.1
  218.3 3.4 %fusion.18 = (bf16[16,16,4,192]{3,2,1,0:T(4,128)(2,1)}, bf16[16,16,4,192]{3,2,1,0:T(4,128)(2,1)S(1)}, bf16[16,16,4,192]{3,2,1,0:T(4,128)(2,1)S(1)}, bf16[16,16,4...) fusion(bf16[18,18,4,192]{3,2,1,0:T(4,128)(2,1)S(1)} %fusion.6), kind=kLoop, calls=%fused_computation.84 | loop fusion | bytes 7077888 | tf_op jit(solution)/shard_map/slice | solution.py:99
  221.7 2.2 reshape.227
  223.9 2.2 reshape.228
  226.1 2.2 reshape.229
  (97 shorter events, 33.7 us)
Async XLA Ops:
  0.0 110.8 %copy-start = (bf16[4,4,128]{2,1,0:T(4,128)(2,1)S(1)}, bf16[4,4,128]{2,1,0:T(4,128)(2,1)}, u32[]{:S(2)}) copy-start(bf16[4,4,128]{2,1,0:T(4,128)(2,1)} %param.15) | copy-start | bytes 12292
  121.9 7.8 %collective-permute-start = (f32[2,20,512]{2,1,0:T(8,128)S(1)}, f32[2,20,512]{2,1,0:T(8,128)S(1)}, u32[]{:S(2)}, u32[]{:S(2)}) collective-permute-start(f32[2,20,512]{2,1,0:T(8,128)S(1)} %get-tuple-element.54), channel_id=1, source_target_pairs={{0,4},{4,8},{8,12},{12,16},{16,20},{20,24},{24,28},{28,32},{32,36}... | collective-permute-start | bytes 245768 | tf_op jit(solution)/shard_map/ppermute | solution.py:13
  127.5 12.2 %collective-permute-start.1 = (f32[2,20,512]{2,1,0:T(8,128)S(1)}, f32[2,20,512]{2,1,0:T(8,128)S(1)}, u32[]{:S(2)}, u32[]{:S(2)}) collective-permute-start(f32[2,20,512]{2,1,0:T(8,128)S(1)} %get-tuple-element.53), channel_id=1, source_target_pairs={{4,0},{8,4},{12,8},{16,12},{20,16},{24,20},{28,24},{32,28},{36,32}... | collective-permute-start | bytes 245768 | tf_op jit(solution)/shard_map/ppermute | solution.py:13
  129.7 36.8 %copy-start.7 = (bf16[3,3,3,32,32]{4,3,2,1,0:T(8,128)(2,1)S(1)}, bf16[3,3,3,32,32]{4,3,2,1,0:T(8,128)(2,1)}, u32[]{:S(2)}) copy-start(bf16[3,3,3,32,32]{4,3,2,1,0:T(8,128)(2,1)} %param.17) | copy-start | bytes 165892
  129.7 36.8 %copy-start.9 = (f32[6,3,4,1,1,1]{0,1,5,4,3,2:T(4,128)S(1)}, f32[6,3,4,1,1,1]{0,1,5,4,3,2:T(4,128)}, u32[]{:S(2)}) copy-start(f32[6,3,4,1,1,1]{0,1,5,4,3,2:T(4,128)} %constant.139) | copy-start | bytes 868
  139.9 5.7 %collective-permute-start.2 = (bf16[16,2,512]{2,1,0:T(2,128)(2,1)S(1)}, bf16[16,2,512]{2,1,0:T(2,128)(2,1)S(1)}, u32[]{:S(2)}, u32[]{:S(2)}) collective-permute-start(bf16[16,2,512]{2,1,0:T(2,128)(2,1)S(1)} %get-tuple-element.74), channel_id=1, source_target_pairs={{0,1},{1,2},{2,3},{4,5},{5,6},{6,7},{8,9},{9,10},{10,11},{12,13},{... | collective-permute-start | bytes 98312 | tf_op jit(solution)/shard_map/ppermute | solution.py:13
  141.9 5.2 %collective-permute-start.3 = (bf16[16,2,512]{2,1,0:T(2,128)(2,1)S(1)}, bf16[16,2,512]{2,1,0:T(2,128)(2,1)S(1)}, u32[]{:S(2)}, u32[]{:S(2)}) collective-permute-start(bf16[16,2,512]{2,1,0:T(2,128)(2,1)S(1)} %get-tuple-element.73), channel_id=1, source_target_pairs={{1,0},{2,1},{3,2},{5,4},{6,5},{7,6},{9,8},{10,9},{11,10},{13,12},{... | collective-permute-start | bytes 98312 | tf_op jit(solution)/shard_map/ppermute | solution.py:13
  147.4 5.9 %collective-permute-start.4 = (bf16[1,16,512]{2,1,0:T(8,128)(2,1)S(1)}, bf16[1,16,512]{2,1,0:T(8,128)(2,1)S(1)}, u32[]{:S(2)}, u32[]{:S(2)}) collective-permute-start(bf16[1,16,512]{2,1,0:T(8,128)(2,1)S(1)} %get-tuple-element.85), channel_id=1, source_target_pairs={{0,4},{4,8},{8,12},{12,16},{16,20},{20,24},{24,28},{28,32},{32,36}... | collective-permute-start | bytes 49160 | tf_op jit(solution)/shard_map/ppermute | solution.py:24
  149.3 11.4 %collective-permute-start.5 = (bf16[1,16,512]{2,1,0:T(8,128)(2,1)S(1)}, bf16[1,16,512]{2,1,0:T(8,128)(2,1)S(1)}, u32[]{:S(2)}, u32[]{:S(2)}) collective-permute-start(bf16[1,16,512]{2,1,0:T(8,128)(2,1)S(1)} %get-tuple-element.86), channel_id=1, source_target_pairs={{4,0},{8,4},{12,8},{16,12},{20,16},{24,20},{28,24},{32,28},{36,32}... | collective-permute-start | bytes 49160 | tf_op jit(solution)/shard_map/ppermute | solution.py:26
  160.7 11.1 %collective-permute-start.6 = (bf16[18,1,512]{2,1,0:T(2,128)(2,1)S(1)}, bf16[18,1,512]{2,1,0:T(2,128)(2,1)S(1)}, u32[]{:S(2)}, u32[]{:S(2)}) collective-permute-start(bf16[18,1,512]{2,1,0:T(2,128)(2,1)S(1)} %get-tuple-element.81), channel_id=1, source_target_pairs={{0,1},{1,2},{2,3},{4,5},{5,6},{6,7},{8,9},{9,10},{10,11},{12,13},{... | collective-permute-start | bytes 55304 | tf_op jit(solution)/shard_map/ppermute | solution.py:24
  162.7 9.2 %collective-permute-start.7 = (bf16[18,1,512]{2,1,0:T(2,128)(2,1)S(1)}, bf16[18,1,512]{2,1,0:T(2,128)(2,1)S(1)}, u32[]{:S(2)}, u32[]{:S(2)}) collective-permute-start(bf16[18,1,512]{2,1,0:T(2,128)(2,1)S(1)} %get-tuple-element.82), channel_id=1, source_target_pairs={{1,0},{2,1},{3,2},{5,4},{6,5},{7,6},{9,8},{10,9},{11,10},{13,12},{... | collective-permute-start | bytes 55304 | tf_op jit(solution)/shard_map/ppermute | solution.py:26
  187.1 2.8 %copy-start.3 = (bf16[1024,192]{1,0:T(8,128)(2,1)S(1)}, bf16[1024,192]{1,0:T(8,128)(2,1)}, u32[]{:S(2)}) copy-start(bf16[1024,192]{1,0:T(8,128)(2,1)} %reshape.218) | copy-start | bytes 1179652
  187.1 2.8 %copy-start.5 = (bf16[3,3,192,128]{3,2,1,0:T(8,128)(2,1)S(1)}, bf16[3,3,192,128]{3,2,1,0:T(8,128)(2,1)}, u32[]{:S(2)}) copy-start(bf16[3,3,192,128]{3,2,1,0:T(8,128)(2,1)} %convert_element_type.81) | copy-start | bytes 1327108
  187.2 3.1 %copy-start.1 = (bf16[1024,192]{1,0:T(8,128)(2,1)S(1)}, bf16[1024,192]{1,0:T(8,128)(2,1)}, u32[]{:S(2)}) copy-start(bf16[1024,192]{1,0:T(8,128)(2,1)} %reshape.219) | copy-start | bytes 1179652
  191.7 19.7 %copy-start.8 = (bf16[3,3,3,32,32]{4,3,2,1,0:T(8,128)(2,1)S(1)}, bf16[3,3,3,32,32]{4,3,2,1,0:T(8,128)(2,1)}, u32[]{:S(2)}) copy-start(bf16[3,3,3,32,32]{4,3,2,1,0:T(8,128)(2,1)} %param.18) | copy-start | bytes 165892
  192.3 5.9 %collective-permute-start.8 = (bf16[1,16,512]{2,1,0:T(8,128)(2,1)S(1)}, bf16[1,16,512]{2,1,0:T(8,128)(2,1)S(1)}, u32[]{:S(2)}, u32[]{:S(2)}) collective-permute-start(bf16[1,16,512]{2,1,0:T(8,128)(2,1)S(1)} %get-tuple-element.83), channel_id=1, source_target_pairs={{0,4},{4,8},{8,12},{12,16},{16,20},{20,24},{24,28},{28,32},{32,36}... | collective-permute-start | bytes 49160 | tf_op jit(solution)/shard_map/ppermute | solution.py:24
  194.2 11.4 %collective-permute-start.9 = (bf16[1,16,512]{2,1,0:T(8,128)(2,1)S(1)}, bf16[1,16,512]{2,1,0:T(8,128)(2,1)S(1)}, u32[]{:S(2)}, u32[]{:S(2)}) collective-permute-start(bf16[1,16,512]{2,1,0:T(8,128)(2,1)S(1)} %get-tuple-element.84), channel_id=1, source_target_pairs={{4,0},{8,4},{12,8},{16,12},{20,16},{24,20},{28,24},{32,28},{36,32}... | collective-permute-start | bytes 49160 | tf_op jit(solution)/shard_map/ppermute | solution.py:26
  205.6 11.2 %collective-permute-start.10 = (bf16[18,1,512]{2,1,0:T(2,128)(2,1)S(1)}, bf16[18,1,512]{2,1,0:T(2,128)(2,1)S(1)}, u32[]{:S(2)}, u32[]{:S(2)}) collective-permute-start(bf16[18,1,512]{2,1,0:T(2,128)(2,1)S(1)} %get-tuple-element.79), channel_id=1, source_target_pairs={{0,1},{1,2},{2,3},{4,5},{5,6},{6,7},{8,9},{9,10},{10,11},{12,13},{... | collective-permute-start | bytes 55304 | tf_op jit(solution)/shard_map/ppermute | solution.py:24
  207.5 9.2 %collective-permute-start.11 = (bf16[18,1,512]{2,1,0:T(2,128)(2,1)S(1)}, bf16[18,1,512]{2,1,0:T(2,128)(2,1)S(1)}, u32[]{:S(2)}, u32[]{:S(2)}) collective-permute-start(bf16[18,1,512]{2,1,0:T(2,128)(2,1)S(1)} %get-tuple-element.80), channel_id=1, source_target_pairs={{1,0},{2,1},{3,2},{5,4},{6,5},{7,6},{9,8},{10,9},{11,10},{13,12},{... | collective-permute-start | bytes 55304 | tf_op jit(solution)/shard_map/ppermute | solution.py:26
  232.0 2.8 %copy-start.4 = (bf16[1024,192]{1,0:T(8,128)(2,1)S(1)}, bf16[1024,192]{1,0:T(8,128)(2,1)}, u32[]{:S(2)}) copy-start(bf16[1024,192]{1,0:T(8,128)(2,1)} %reshape.229) | copy-start | bytes 1179652
  232.0 2.8 %copy-start.6 = (bf16[3,3,192,128]{3,2,1,0:T(8,128)(2,1)S(1)}, bf16[3,3,192,128]{3,2,1,0:T(8,128)(2,1)}, u32[]{:S(2)}) copy-start(bf16[3,3,192,128]{3,2,1,0:T(8,128)(2,1)} %convert_element_type.85) | copy-start | bytes 1327108
  232.1 3.1 %copy-start.2 = (bf16[1024,192]{1,0:T(8,128)(2,1)S(1)}, bf16[1024,192]{1,0:T(8,128)(2,1)}, u32[]{:S(2)}) copy-start(bf16[1024,192]{1,0:T(8,128)(2,1)} %reshape.230) | copy-start | bytes 1179652
where the time goes:
time: 240 us; the launch traced here: 238 us
  local copies, waits for them, and re-layouts  116 us (48%)
  matrix products  54.2 us (23%)
  starting transfers between devices  36.3 us (15%)
  waiting for transfers between devices  26.5 us (11%)
  other arithmetic  3.8 us (2%)
    convert_element_type x3, local copies, waits for them, and re-layouts, up_tables(): placed.reshape(2, 2, coarse_depth * channels, 16 * fine_depth * channels)  79.8 us
    dot_general x1, matrix products, up_tables(): jnp.einsum('akf,ijkcd->ijacfd', jnp.asarray(tap_table), up_weight.astype(...  30.9 us
    reshape x18, local copies, waits for them, and re-layouts, refine(): window.reshape(-1, 6 * channels)  20.5 us
    ppermute x4, starting transfers between devices, extended_2(): lax.ppermute(head, axis, [((i + 1) % count, i) for i in range(ends)])  15.5 us
    ppermute x4, waiting for transfers between devices, extended_2(): lax.ppermute(head, axis, [((i + 1) % count, i) for i in range(ends)])  14.8 us
    ppermute x4, starting transfers between devices, passed_along(): return lax.ppermute(block, axis, route)  13.1 us
    ppermute x4, waiting for transfers between devices, passed_along(): return lax.ppermute(block, axis, route)  11.7 us
    dot_general x18, matrix products, refine(): jnp.dot(window.reshape(-1, 6 * channels), band_mats[shift_one, shift_two]...  9.55 us
  transfers between devices with their start and end apart: 12, of which 5 were waited for; matrix products, arithmetic and copies ran while one was open for 5% of the time, Pallas kernels for 0%

commit v1 on v0

--- a/solution.py
+++ b/solution.py
@@ -33,36 +33,29 @@
 def up_tables(up_weight, coarse_depth):
     channels = up_weight.shape[3]
     fine_depth = 4 * coarse_depth
-    coarse_pos = np.arange(coarse_depth)[:, None, None]
-    kernel_pos = np.arange(8)[None, :, None]
-    fine_pos = np.arange(fine_depth)[None, None, :]
-    tap_table = (4 * coarse_pos + kernel_pos - 2 == fine_pos).astype(np.float32)
-    placed = jnp.einsum(
-        "akf,ijkcd->ijacfd",
-        jnp.asarray(tap_table),
-        up_weight.astype(jnp.float32),
-        precision=HIGHEST,
+    zero = jnp.zeros((), up_weight.dtype)
+    taps = up_weight.reshape(2, 4, 2, 4, 8, channels, channels).transpose(0, 2, 5, 1, 3, 4, 6)
+    keep = [(0, 0, 0)] * 5
+    placed = jnp.stack(
+        [
+            lax.pad(taps, zero, keep + [(4 * c - 2, fine_depth - 4 * c - 6, 0), (0, 0, 0)])
+            for c in range(coarse_depth)
+        ],
+        axis=2,
     )
-    placed = placed.reshape(2, 4, 2, 4, coarse_depth * channels, fine_depth * channels)
-    placed = placed.transpose(0, 2, 4, 1, 3, 5)
-    return placed.reshape(2, 2, coarse_depth * channels, 16 * fine_depth * channels).astype(
-        jnp.bfloat16
-    )
+    return placed.reshape(2, 2, coarse_depth * channels, 16 * fine_depth * channels)
 
 
 def band_tables(weight):
     channels = weight.shape[3]
-    cells_in = np.array([0, 1, 2, 3, -1, 4])
-    tap_table = (
-        cells_in[:, None, None] == np.arange(4)[None, None, :] + np.arange(3)[None, :, None] - 1
+    zero = jnp.zeros((), weight.dtype)
+    keep = [(0, 0, 0)] * 2
+    natural = jnp.stack(
+        [lax.pad(weight, zero, keep + [(o, 3 - o, 0), (0, 0, 0), (0, 0, 0)]) for o in range(4)],
+        axis=4,
     )
-    band_mats = jnp.einsum(
-        "rdo,xydce->xyrcoe",
-        jnp.asarray(tap_table.astype(np.float32)),
-        weight.astype(jnp.float32),
-        precision=HIGHEST,
-    )
-    return band_mats.reshape(3, 3, 6 * channels, 4 * channels).astype(jnp.bfloat16)
+    band_mats = jnp.concatenate([natural[:, :, 1:5], natural[:, :, 0:1], natural[:, :, 5:6]], axis=2)
+    return band_mats.reshape(3, 3, 6 * channels, 4 * channels)
 
 
 def spread(coarse_block, up_mats):

time: 240 us -> 218 us (0.908)
  matrix products: 54.2 us -> 19.3 us
  other arithmetic: 3.8 us -> 31.6 us
  local copies, waits for them, and re-layouts: 116 us -> 103 us
    convert_element_type x7 -> x0, local copies, waits for them, and re-layouts: 85.8 us -> none  [the longest x3 79.8 us: up_tables(): placed.reshape(2, 2, coarse_depth * channels, 16 * fine_depth * channels)]
    reshape x0 -> x4, local copies, waits for them, and re-layouts: none -> 48.7 us  [the longest x1 41.6 us: up_tables(): placed.reshape(2, 2, coarse_depth * channels, 16 * fine_depth * channels)]
    dot_general x3 -> x0, matrix products: 35.6 us -> none  [the longest x1 30.9 us: up_tables(): jnp.einsum('akf,ijkcd->ijacfd', jnp.asarray(tap_table), up_weight.astype(...]
    another operation x1 -> x4, other arithmetic: 0.05 us -> 24.1 us  [the longest x1 23.1 us: up_tables(): jnp.stack([lax.pad(taps, zero, keep + [(4 * c - 2, fine_depth - 4 * c - 6...]
    another operation x0 -> x3, local copies, waits for them, and re-layouts: none -> 14.1 us  [the longest x1 12.6 us: up_tables(): jnp.stack([lax.pad(taps, zero, keep + [(4 * c - 2, fine_depth - 4 * c - 6...]
    concatenate x0 -> x2, local copies, waits for them, and re-layouts: none -> 3.85 us  [band_tables(): jnp.concatenate([natural[:, :, 1:5], natural[:, :, 0:1], natural[:, :, 5:...]
    reshape x18, local copies, waits for them, and re-layouts: 20.5 us -> 24.1 us  [refine(): window.reshape(-1, 6 * channels)]
  transfers between devices with their start and end apart: 12 -> 12, of which waited for: 5 -> 4; matrix products, arithmetic and copies ran while one was open for 5% -> 5% of each run, Pallas kernels for 0% -> 0%
where the time goes in v1:
time: 218 us; the launch traced here: 216 us
  local copies, waits for them, and re-layouts  103 us (47%)
  starting transfers between devices  36.4 us (17%)
  other arithmetic  31.6 us (14%)
  waiting for transfers between devices  25.1 us (12%)
  matrix products  19.3 us (9%)
    reshape x1, local copies, waits for them, and re-layouts, up_tables(): placed.reshape(2, 2, coarse_depth * channels, 16 * fine_depth * channels)  41.6 us
    reshape x18, local copies, waits for them, and re-layouts, refine(): window.reshape(-1, 6 * channels)  24.1 us
    another operation x1, other arithmetic, up_tables(): jnp.stack([lax.pad(taps, zero, keep + [(4 * c - 2, fine_depth - 4 * c - 6...  23.1 us
    ppermute x4, starting transfers between devices, extended_2(): lax.ppermute(head, axis, [((i + 1) % count, i) for i in range(ends)])  15.7 us
    ppermute x4, waiting for transfers between devices, extended_2(): lax.ppermute(head, axis, [((i + 1) % count, i) for i in range(ends)])  13.6 us
    ppermute x4, starting transfers between devices, passed_along(): return lax.ppermute(block, axis, route)  13.1 us
    another operation x1, local copies, waits for them, and re-layouts, up_tables(): jnp.stack([lax.pad(taps, zero, keep + [(4 * c - 2, fine_depth - 4 * c - 6...  12.6 us
    ppermute x4, waiting for transfers between devices, passed_along(): return lax.ppermute(block, axis, route)  11.4 us
  transfers between devices with their start and end apart: 12, of which 4 were waited for; matrix products, arithmetic and copies ran while one was open for 5% of the time, Pallas kernels for 0%

profile of v1, /device:TPU:126, one launch (start us, length us, event | category | flops | bytes accessed | tf_op | source)
XLA Modules:
  0.0 215.6 jit_solution(7263066850616884628)
XLA Ops:
  0.0 3.8 %copy.14 = bf16[2,4,2,4,8,32,32]{6,4,3,1,5,2,0:T(8,128)(2,1)S(1)} copy(bf16[2,4,2,4,8,32,32]{6,5,4,3,2,1,0:T(8,128)(2,1)} %bitcast.140) | data formatting | bytes 2097152 | tf_op jit(solution)/shard_map/reshape | solution.py:37
  3.8 12.6 %fusion = (bf16[2,2,1,32,4,4,16,32]{7,6,5,4,3,2,1,0:T(8,128)(2,1)}, bf16[2,2,1,32,4,4,16,32]{7,6,5,4,3,2,1,0:T(8,128)(2,1)}, bf16[2,2,1,32,4,4,16,32]{7,6,5,4,3,...) fusion(bf16[2,2,32,4,4,8,32]{6,5,4,3,2,1,0:T(8,128)(2,1)S(1)} %bitcast.139), kind=kLoop, calls=%fused_computation.7 | loop fusion | bytes 9437184 | tf_op jit(solution)/shard_map/stack | solution.py:39
  16.4 23.1 %pad_maximum_fusion = bf16[2,2,4,32,4,4,16,32]{7,6,5,4,3,2,1,0:T(8,128)(2,1)} fusion(bf16[2,2,1,32,4,4,16,32]{7,6,5,4,3,2,1,0:T(8,128)(2,1)} %get-tuple-element.54, bf16[2,2,1,32,4,4,16,32]{7,6,5,4,3,2,1,0:T(8,128)(2,1)} %get-tuple-element.55, bf16[2,2,1,32,4,4,16,32]{7,6,5,4,3,2,1,0:T(8,128)(2,1)} %get-tuple-element.56, ...), kind=kLoop, calls=%fused_computation | loop fusion | flops 12582912 | bytes 16777216 | tf_op jit(solution)/shard_map/stack | solution.py:39
  39.5 41.6 %reshape.214 = bf16[2,2,128,8192]{3,2,1,0:T(8,128)(2,1)} reshape(bf16[2,2,4,32,4,4,16,32]{7,6,5,4,3,2,1,0:T(8,128)(2,1)} %pad_maximum_fusion) | data formatting | bytes 16777216 | tf_op jit(solution)/shard_map/reshape | solution.py:46
  81.2 2.0 convolution_bitcast_fusion.3
  83.1 2.0 convolution_bitcast_fusion.2
  85.1 2.0 convolution_bitcast_fusion.1
  87.1 2.0 convolution_bitcast_fusion
  91.2 5.6 %collective-permute-start = (f32[2,20,512]{2,1,0:T(8,128)S(1)}, f32[2,20,512]{2,1,0:T(8,128)S(1)}, u32[]{:S(2)}, u32[]{:S(2)}) collective-permute-start(f32[2,20,512]{2,1,0:T(8,128)S(1)} %get-tuple-element.58), channel_id=1, source_target_pairs={{0,4},{4,8},{8,12},{12,16},{16,20},{20,24},{24,28},{28,32},{32,36}... | collective-permute-start | bytes 245768 | tf_op jit(solution)/shard_map/ppermute | solution.py:13
  96.8 1.9 collective-permute-start.1
  99.1 10.0 %collective-permute-done.1 = f32[2,20,512]{2,1,0:T(8,128)S(1)} collective-permute-done((f32[2,20,512]{2,1,0:T(8,128)S(1)}, f32[2,20,512]{2,1,0:T(8,128)S(1)}, u32[]{:S(2)}, u32[]{:S(2)}) %collective-permute-start.1) | collective-permute-done | bytes 81952 | tf_op jit(solution)/shard_map/ppermute | solution.py:13
  109.2 1.9 collective-permute-start.2
  111.9 3.6 %collective-permute-start.3 = (bf16[16,2,512]{2,1,0:T(2,128)(2,1)S(1)}, bf16[16,2,512]{2,1,0:T(2,128)(2,1)S(1)}, u32[]{:S(2)}, u32[]{:S(2)}) collective-permute-start(bf16[16,2,512]{2,1,0:T(2,128)(2,1)S(1)} %get-tuple-element.77), channel_id=1, source_target_pairs={{1,0},{2,1},{3,2},{5,4},{6,5},{7,6},{9,8},{10,9},{11,10},{13,12},{... | collective-permute-start | bytes 98312 | tf_op jit(solution)/shard_map/ppermute | solution.py:13
  117.4 1.9 collective-permute-start.4
  119.4 4.1 %collective-permute-start.5 = (bf16[1,16,512]{2,1,0:T(8,128)(2,1)S(1)}, bf16[1,16,512]{2,1,0:T(8,128)(2,1)S(1)}, u32[]{:S(2)}, u32[]{:S(2)}) collective-permute-start(bf16[1,16,512]{2,1,0:T(8,128)(2,1)S(1)} %get-tuple-element.90), channel_id=1, source_target_pairs={{4,0},{8,4},{12,8},{16,12},{20,16},{24,20},{28,24},{32,28},{36,32}... | collective-permute-start | bytes 49160 | tf_op jit(solution)/shard_map/ppermute | solution.py:26
  123.9 6.9 %collective-permute-done.5 = bf16[1,16,512]{2,1,0:T(8,128)(2,1)S(1)} collective-permute-done((bf16[1,16,512]{2,1,0:T(8,128)(2,1)S(1)}, bf16[1,16,512]{2,1,0:T(8,128)(2,1)S(1)}, u32[]{:S(2)}, u32[]{:S(2)}) %collective-permute-start.5) | collective-permute-done | bytes 16416 | tf_op jit(solution)/shard_map/ppermute | solution.py:26
  133.4 3.8 %collective-permute-start.7 = (bf16[18,1,512]{2,1,0:T(2,128)(2,1)S(1)}, bf16[18,1,512]{2,1,0:T(2,128)(2,1)}, u32[]{:S(2)}, u32[]{:S(2)}) collective-permute-start(bf16[18,1,512]{2,1,0:T(2,128)(2,1)S(1)} %get-tuple-element.86), channel_id=1, source_target_pairs={{1,0},{2,1},{3,2},{5,4},{6,5},{7,6},{9,8},{10,9},{11,10},{13,12},{... | collective-permute-start | bytes 55304 | tf_op jit(solution)/shard_map/ppermute | solution.py:26
  138.5 1.9 copy.11
  144.4 3.6 %fusion.35 = (bf16[16,16,4,192]{3,2,1,0:T(4,128)(2,1)}, bf16[16,16,4,192]{3,2,1,0:T(4,128)(2,1)}, bf16[16,16,4,192]{3,2,1,0:T(4,128)(2,1)S(1)}, bf16[16,16,4,192...) fusion(bf16[18,18,4,192]{3,2,1,0:T(4,128)(2,1)S(1)} %fusion.25), kind=kLoop, calls=%fused_computation.127 | loop fusion | bytes 7077888 | tf_op jit(solution)/shard_map/slice | solution.py:92
  147.9 2.2 %reshape.222 = bf16[1024,192]{1,0:T(8,128)(2,1)} reshape(bf16[16,16,4,192]{3,2,1,0:T(4,128)(2,1)} %get-tuple-element.76) | data formatting | bytes 786432 | tf_op jit(solution)/shard_map/reshape | solution.py:94
  150.1 2.1 reshape.224
  152.2 2.2 reshape.225
  154.4 2.2 %reshape.226 = bf16[1024,192]{1,0:T(8,128)(2,1)} reshape(bf16[16,16,4,192]{3,2,1,0:T(4,128)(2,1)} %get-tuple-element.73) | data formatting | bytes 786432 | tf_op jit(solution)/shard_map/reshape | solution.py:94
  159.7 2.1 reshape.231
  171.9 3.9 %collective-permute-start.9 = (bf16[1,16,512]{2,1,0:T(8,128)(2,1)S(1)}, bf16[1,16,512]{2,1,0:T(8,128)(2,1)S(1)}, u32[]{:S(2)}, u32[]{:S(2)}) collective-permute-start(bf16[1,16,512]{2,1,0:T(8,128)(2,1)S(1)} %get-tuple-element.88), channel_id=1, source_target_pairs={{4,0},{8,4},{12,8},{16,12},{20,16},{24,20},{28,24},{32,28},{36,32}... | collective-permute-start | bytes 49160 | tf_op jit(solution)/shard_map/ppermute | solution.py:26
  176.6 6.7 %collective-permute-done.9 = bf16[1,16,512]{2,1,0:T(8,128)(2,1)S(1)} collective-permute-done((bf16[1,16,512]{2,1,0:T(8,128)(2,1)S(1)}, bf16[1,16,512]{2,1,0:T(8,128)(2,1)S(1)}, u32[]{:S(2)}, u32[]{:S(2)}) %collective-permute-start.9) | collective-permute-done | bytes 16416 | tf_op jit(solution)/shard_map/ppermute | solution.py:26
  185.9 3.9 %collective-permute-start.11 = (bf16[18,1,512]{2,1,0:T(2,128)(2,1)S(1)}, bf16[18,1,512]{2,1,0:T(2,128)(2,1)}, u32[]{:S(2)}, u32[]{:S(2)}) collective-permute-start(bf16[18,1,512]{2,1,0:T(2,128)(2,1)S(1)} %get-tuple-element.84), channel_id=1, source_target_pairs={{1,0},{2,1},{3,2},{5,4},{6,5},{7,6},{9,8},{10,9},{11,10},{13,12},{... | collective-permute-start | bytes 55304 | tf_op jit(solution)/shard_map/ppermute | solution.py:26
  190.2 1.9 copy.12
  196.1 3.5 %fusion.34 = (bf16[16,16,4,192]{3,2,1,0:T(4,128)(2,1)}, bf16[16,16,4,192]{3,2,1,0:T(4,128)(2,1)S(1)}, bf16[16,16,4,192]{3,2,1,0:T(4,128)(2,1)S(1)}, bf16[16,16,4...) fusion(bf16[18,18,4,192]{3,2,1,0:T(4,128)(2,1)S(1)} %fusion.26), kind=kLoop, calls=%fused_computation.126 | loop fusion | bytes 7077888 | tf_op jit(solution)/shard_map/slice | solution.py:92
  199.5 2.2 %reshape.234 = bf16[1024,192]{1,0:T(8,128)(2,1)} reshape(bf16[16,16,4,192]{3,2,1,0:T(4,128)(2,1)} %get-tuple-element.67) | data formatting | bytes 786432 | tf_op jit(solution)/shard_map/reshape | solution.py:94
  201.7 2.1 reshape.236
  203.9 2.2 %reshape.237 = bf16[1024,192]{1,0:T(8,128)(2,1)} reshape(bf16[16,16,4,192]{3,2,1,0:T(4,128)(2,1)} %get-tuple-element.65) | data formatting | bytes 786432 | tf_op jit(solution)/shard_map/reshape | solution.py:94
  (109 shorter events, 43.5 us)
Async XLA Ops:
  0.0 81.2 %copy-start = (bf16[4,4,128]{2,1,0:T(4,128)(2,1)S(1)}, bf16[4,4,128]{2,1,0:T(4,128)(2,1)}, u32[]{:S(2)}) copy-start(bf16[4,4,128]{2,1,0:T(4,128)(2,1)} %param.12) | copy-start | bytes 12292
  90.9 7.9 %copy-start.11 = (bf16[3,3,3,32,32]{4,3,2,1,0:T(8,128)(2,1)S(1)}, bf16[3,3,3,32,32]{4,3,2,1,0:T(8,128)(2,1)}, u32[]{:S(2)}) copy-start(bf16[3,3,3,32,32]{4,3,2,1,0:T(8,128)(2,1)} %param.14) | copy-start | bytes 165892
  91.2 7.9 %collective-permute-start = (f32[2,20,512]{2,1,0:T(8,128)S(1)}, f32[2,20,512]{2,1,0:T(8,128)S(1)}, u32[]{:S(2)}, u32[]{:S(2)}) collective-permute-start(f32[2,20,512]{2,1,0:T(8,128)S(1)} %get-tuple-element.58), channel_id=1, source_target_pairs={{0,4},{4,8},{8,12},{12,16},{16,20},{20,24},{24,28},{28,32},{32,36}... | collective-permute-start | bytes 245768 | tf_op jit(solution)/shard_map/ppermute | solution.py:13
  96.8 12.2 %collective-permute-start.1 = (f32[2,20,512]{2,1,0:T(8,128)S(1)}, f32[2,20,512]{2,1,0:T(8,128)S(1)}, u32[]{:S(2)}, u32[]{:S(2)}) collective-permute-start(f32[2,20,512]{2,1,0:T(8,128)S(1)} %get-tuple-element.57), channel_id=1, source_target_pairs={{4,0},{8,4},{12,8},{16,12},{20,16},{24,20},{28,24},{32,28},{36,32}... | collective-permute-start | bytes 245768 | tf_op jit(solution)/shard_map/ppermute | solution.py:13
  109.2 6.4 %collective-permute-start.2 = (bf16[16,2,512]{2,1,0:T(2,128)(2,1)S(1)}, bf16[16,2,512]{2,1,0:T(2,128)(2,1)S(1)}, u32[]{:S(2)}, u32[]{:S(2)}) collective-permute-start(bf16[16,2,512]{2,1,0:T(2,128)(2,1)S(1)} %get-tuple-element.78), channel_id=1, source_target_pairs={{0,1},{1,2},{2,3},{4,5},{5,6},{6,7},{8,9},{9,10},{10,11},{12,13},{... | collective-permute-start | bytes 98312 | tf_op jit(solution)/shard_map/ppermute | solution.py:13
  111.9 5.2 %collective-permute-start.3 = (bf16[16,2,512]{2,1,0:T(2,128)(2,1)S(1)}, bf16[16,2,512]{2,1,0:T(2,128)(2,1)S(1)}, u32[]{:S(2)}, u32[]{:S(2)}) collective-permute-start(bf16[16,2,512]{2,1,0:T(2,128)(2,1)S(1)} %get-tuple-element.77), channel_id=1, source_target_pairs={{1,0},{2,1},{3,2},{5,4},{6,5},{7,6},{9,8},{10,9},{11,10},{13,12},{... | collective-permute-start | bytes 98312 | tf_op jit(solution)/shard_map/ppermute | solution.py:13
  117.4 6.5 %collective-permute-start.4 = (bf16[1,16,512]{2,1,0:T(8,128)(2,1)S(1)}, bf16[1,16,512]{2,1,0:T(8,128)(2,1)S(1)}, u32[]{:S(2)}, u32[]{:S(2)}) collective-permute-start(bf16[1,16,512]{2,1,0:T(8,128)(2,1)S(1)} %get-tuple-element.89), channel_id=1, source_target_pairs={{0,4},{4,8},{8,12},{12,16},{16,20},{20,24},{24,28},{28,32},{32,36}... | collective-permute-start | bytes 49160 | tf_op jit(solution)/shard_map/ppermute | solution.py:24
  119.4 17.9 %copy-start.12 = (bf16[3,3,3,32,32]{4,3,2,1,0:T(8,128)(2,1)S(1)}, bf16[3,3,3,32,32]{4,3,2,1,0:T(8,128)(2,1)}, u32[]{:S(2)}) copy-start(bf16[3,3,3,32,32]{4,3,2,1,0:T(8,128)(2,1)} %param.15) | copy-start | bytes 165892
  119.4 11.5 %collective-permute-start.5 = (bf16[1,16,512]{2,1,0:T(8,128)(2,1)S(1)}, bf16[1,16,512]{2,1,0:T(8,128)(2,1)S(1)}, u32[]{:S(2)}, u32[]{:S(2)}) collective-permute-start(bf16[1,16,512]{2,1,0:T(8,128)(2,1)S(1)} %get-tuple-element.90), channel_id=1, source_target_pairs={{4,0},{8,4},{12,8},{16,12},{20,16},{24,20},{28,24},{32,28},{36,32}... | collective-permute-start | bytes 49160 | tf_op jit(solution)/shard_map/ppermute | solution.py:26
  131.5 10.5 %collective-permute-start.6 = (bf16[18,1,512]{2,1,0:T(2,128)(2,1)}, bf16[18,1,512]{2,1,0:T(2,128)(2,1)S(1)}, u32[]{:S(2)}, u32[]{:S(2)}) collective-permute-start(bf16[18,1,512]{2,1,0:T(2,128)(2,1)} %get-tuple-element.85), channel_id=1, source_target_pairs={{0,1},{1,2},{2,3},{4,5},{5,6},{6,7},{8,9},{9,10},{10,11},{12,13},{... | collective-permute-start | bytes 55304 | tf_op jit(solution)/shard_map/ppermute | solution.py:24
  133.4 8.6 %collective-permute-start.7 = (bf16[18,1,512]{2,1,0:T(2,128)(2,1)S(1)}, bf16[18,1,512]{2,1,0:T(2,128)(2,1)}, u32[]{:S(2)}, u32[]{:S(2)}) collective-permute-start(bf16[18,1,512]{2,1,0:T(2,128)(2,1)S(1)} %get-tuple-element.86), channel_id=1, source_target_pairs={{1,0},{2,1},{3,2},{5,4},{6,5},{7,6},{9,8},{10,9},{11,10},{13,12},{... | collective-permute-start | bytes 55304 | tf_op jit(solution)/shard_map/ppermute | solution.py:26
  161.8 4.1 %copy-start.6 = (bf16[1024,192]{1,0:T(8,128)(2,1)S(1)}, bf16[1024,192]{1,0:T(8,128)(2,1)}, u32[]{:S(2)}) copy-start(bf16[1024,192]{1,0:T(8,128)(2,1)} %reshape.226) | copy-start | bytes 1179652
  161.8 4.2 %copy-start.9 = (bf16[3,3,192,128]{3,2,1,0:T(8,128)(2,1)S(1)}, bf16[3,3,192,128]{3,2,1,0:T(8,128)(2,1)}, u32[]{:S(2)}) copy-start(bf16[3,3,192,128]{3,2,1,0:T(8,128)(2,1)} %reshape.223) | copy-start | bytes 1327108
  163.2 3.0 %copy-start.5 = (bf16[1024,192]{1,0:T(8,128)(2,1)S(1)}, bf16[1024,192]{1,0:T(8,128)(2,1)}, u32[]{:S(2)}) copy-start(bf16[1024,192]{1,0:T(8,128)(2,1)} %reshape.227) | copy-start | bytes 1179652
  166.6 1.0 copy-start.4
  167.6 8.2 %copy-start.2 = (bf16[3,3,6,32,1,32]{5,3,2,1,0,4:T(8,128)(2,1)S(1)}, bf16[3,3,6,32,1,32]{5,3,2,1,0,4:T(8,128)(2,1)}, u32[]{:S(2)}) copy-start(bf16[3,3,6,32,1,32]{5,3,2,1,0,4:T(8,128)(2,1)} %get-tuple-element.93) | copy-start | bytes 331780
  167.6 8.3 %copy-start.3 = (bf16[3,3,6,32,1,32]{5,3,2,1,0,4:T(8,128)(2,1)S(1)}, bf16[3,3,6,32,1,32]{5,3,2,1,0,4:T(8,128)(2,1)}, u32[]{:S(2)}) copy-start(bf16[3,3,6,32,1,32]{5,3,2,1,0,4:T(8,128)(2,1)} %get-tuple-element.94) | copy-start | bytes 331780
  170.0 6.6 %collective-permute-start.8 = (bf16[1,16,512]{2,1,0:T(8,128)(2,1)S(1)}, bf16[1,16,512]{2,1,0:T(8,128)(2,1)S(1)}, u32[]{:S(2)}, u32[]{:S(2)}) collective-permute-start(bf16[1,16,512]{2,1,0:T(8,128)(2,1)S(1)} %get-tuple-element.87), channel_id=1, source_target_pairs={{0,4},{4,8},{8,12},{12,16},{16,20},{20,24},{24,28},{28,32},{32,36}... | collective-permute-start | bytes 49160 | tf_op jit(solution)/shard_map/ppermute | solution.py:24
  171.9 11.4 %collective-permute-start.9 = (bf16[1,16,512]{2,1,0:T(8,128)(2,1)S(1)}, bf16[1,16,512]{2,1,0:T(8,128)(2,1)S(1)}, u32[]{:S(2)}, u32[]{:S(2)}) collective-permute-start(bf16[1,16,512]{2,1,0:T(8,128)(2,1)S(1)} %get-tuple-element.88), channel_id=1, source_target_pairs={{4,0},{8,4},{12,8},{16,12},{20,16},{24,20},{28,24},{32,28},{36,32}... | collective-permute-start | bytes 49160 | tf_op jit(solution)/shard_map/ppermute | solution.py:26
  184.0 9.8 %collective-permute-start.10 = (bf16[18,1,512]{2,1,0:T(2,128)(2,1)}, bf16[18,1,512]{2,1,0:T(2,128)(2,1)S(1)}, u32[]{:S(2)}, u32[]{:S(2)}) collective-permute-start(bf16[18,1,512]{2,1,0:T(2,128)(2,1)} %get-tuple-element.83), channel_id=1, source_target_pairs={{0,1},{1,2},{2,3},{4,5},{5,6},{6,7},{8,9},{9,10},{10,11},{12,13},{... | collective-permute-start | bytes 55304 | tf_op jit(solution)/shard_map/ppermute | solution.py:24
  185.9 7.9 %collective-permute-start.11 = (bf16[18,1,512]{2,1,0:T(2,128)(2,1)S(1)}, bf16[18,1,512]{2,1,0:T(2,128)(2,1)}, u32[]{:S(2)}, u32[]{:S(2)}) collective-permute-start(bf16[18,1,512]{2,1,0:T(2,128)(2,1)S(1)} %get-tuple-element.84), channel_id=1, source_target_pairs={{1,0},{2,1},{3,2},{5,4},{6,5},{7,6},{9,8},{10,9},{11,10},{13,12},{... | collective-permute-start | bytes 55304 | tf_op jit(solution)/shard_map/ppermute | solution.py:26
  209.8 2.8 %copy-start.8 = (bf16[1024,192]{1,0:T(8,128)(2,1)S(1)}, bf16[1024,192]{1,0:T(8,128)(2,1)}, u32[]{:S(2)}) copy-start(bf16[1024,192]{1,0:T(8,128)(2,1)} %reshape.237) | copy-start | bytes 1179652
  209.8 2.8 %copy-start.10 = (bf16[3,3,192,128]{3,2,1,0:T(8,128)(2,1)S(1)}, bf16[3,3,192,128]{3,2,1,0:T(8,128)(2,1)}, u32[]{:S(2)}) copy-start(bf16[3,3,192,128]{3,2,1,0:T(8,128)(2,1)} %reshape.235) | copy-start | bytes 1327108
  209.8 3.1 %copy-start.7 = (bf16[1024,192]{1,0:T(8,128)(2,1)S(1)}, bf16[1024,192]{1,0:T(8,128)(2,1)}, u32[]{:S(2)}) copy-start(bf16[1024,192]{1,0:T(8,128)(2,1)} %reshape.238) | copy-start | bytes 1179652
  214.1 1.5 copy-start.1

commit v2 on v1

--- a/solution.py
+++ b/solution.py
@@ -34,16 +34,20 @@
     channels = up_weight.shape[3]
     fine_depth = 4 * coarse_depth
     zero = jnp.zeros((), up_weight.dtype)
-    taps = up_weight.reshape(2, 4, 2, 4, 8, channels, channels).transpose(0, 2, 5, 1, 3, 4, 6)
+    taps = up_weight.reshape(2, 4, 2, 4, 8, channels, channels).transpose(0, 2, 1, 3, 5, 4, 6)
+    taps = taps.reshape(2, 2, 4, 4, channels, 8 * channels)
     keep = [(0, 0, 0)] * 5
-    placed = jnp.stack(
+    return jnp.concatenate(
         [
-            lax.pad(taps, zero, keep + [(4 * c - 2, fine_depth - 4 * c - 6, 0), (0, 0, 0)])
+            lax.pad(
+                taps,
+                zero,
+                keep + [(channels * (4 * c - 2), channels * (fine_depth - 4 * c - 6), 0)],
+            )
             for c in range(coarse_depth)
         ],
-        axis=2,
+        axis=4,
     )
-    return placed.reshape(2, 2, coarse_depth * channels, 16 * fine_depth * channels)
 
 
 def band_tables(weight):
@@ -60,20 +64,24 @@
 
 def spread(coarse_block, up_mats):
     size_one, size_two, depth_lanes = coarse_block.shape
-    lane_width = up_mats.shape[3] // 16
+    lane_width = up_mats.shape[5]
     flat_rows = coarse_block.reshape(size_one * size_two, depth_lanes)
-    summed = jnp.zeros((size_one + 1, size_two + 1, 4, 4, lane_width), jnp.float32)
+    stacked = up_mats.reshape(64, depth_lanes, lane_width)
+    product = jnp.einsum(
+        "bpk,bkn->bpn",
+        jnp.broadcast_to(flat_rows, (64,) + flat_rows.shape),
+        stacked,
+        preferred_element_type=jnp.float32,
+    )
+    product = product.reshape(2, 2, 4, 4, size_one, size_two, lane_width)
+    summed = jnp.zeros((4, 4, size_one + 1, size_two + 1, lane_width), jnp.float32)
     for high_one in (0, 1):
         for high_two in (0, 1):
-            product = jnp.dot(
-                flat_rows, up_mats[high_one, high_two], preferred_element_type=jnp.float32
+            summed = summed + jnp.pad(
+                product[high_one, high_two],
+                ((0, 0), (0, 0), (high_one, 1 - high_one), (high_two, 1 - high_two), (0, 0)),
             )
-            product = product.reshape(size_one, size_two, 4, 4, lane_width)
-            summed = summed + jnp.pad(
-                product,
-                ((high_one, 1 - high_one), (high_two, 1 - high_two), (0, 0), (0, 0), (0, 0)),
-            )
-    summed = summed.transpose(0, 2, 1, 3, 4)
+    summed = summed.transpose(2, 0, 3, 1, 4)
     return summed.reshape(4 * size_one + 4, 4 * size_two + 4, lane_width)
 
 

time: 218 us -> 146 us (0.67)
  local copies, waits for them, and re-layouts: 103 us -> 59.9 us
  other arithmetic: 31.6 us -> 11.6 us
  matrix products: 19.3 us -> 10.8 us
    reshape x6 -> x2, local copies, waits for them, and re-layouts: 46.8 us -> 7.01 us  [the longest x1 5.33 us: up_tables(): taps = taps.reshape(2, 2, 4, 4, channels, 8 * channels)]
    another operation x2 -> x1, other arithmetic: 23.1 us -> 0.05 us  [the longest x1 23.1 us: up_tables(): jnp.stack([lax.pad(taps, zero, keep + [(4 * c - 2, fine_depth - 4 * c - 6...]
    another operation x1 -> x0, local copies, waits for them, and re-layouts: 12.6 us -> none  [up_tables(): jnp.stack([lax.pad(taps, zero, keep + [(4 * c - 2, fine_depth - 4 * c - 6...]
    transpose x1 -> x2, local copies, waits for them, and re-layouts: 0.05 us -> 8.95 us  [the longest x1 8.34 us: up_tables(): up_weight.reshape(2, 4, 2, 4, 8, channels, channels)]
    dot_general x4 -> x1, matrix products: 7.92 us -> 1.2 us  [spread(): jnp.einsum('bpk,bkn->bpn', jnp.broadcast_to(flat_rows, (64,) + flat_rows....]
  transfers between devices with their start and end apart: 12 -> 12, of which waited for: 4 -> 4; matrix products, arithmetic and copies ran while one was open for 5% -> 8% of each run, Pallas kernels for 0% -> 0%
where the time goes in v2:
time: 146 us; the launch traced here: 144 us
  local copies, waits for them, and re-layouts  59.9 us (41%)
  starting transfers between devices  36.2 us (25%)
  waiting for transfers between devices  25 us (17%)
  other arithmetic  11.6 us (8%)
  matrix products  10.8 us (7%)
    reshape x18, local copies, waits for them, and re-layouts, refine(): window.reshape(-1, 6 * channels)  22.3 us
    ppermute x4, starting transfers between devices, extended_2(): lax.ppermute(head, axis, [((i + 1) % count, i) for i in range(ends)])  15.5 us
    ppermute x4, waiting for transfers between devices, extended_2(): lax.ppermute(head, axis, [((i + 1) % count, i) for i in range(ends)])  13.6 us
    ppermute x4, starting transfers between devices, passed_along(): return lax.ppermute(block, axis, route)  13.1 us
    ppermute x4, waiting for transfers between devices, passed_along(): return lax.ppermute(block, axis, route)  11.4 us
    dot_general x18, matrix products, refine(): jnp.dot(window.reshape(-1, 6 * channels), band_mats[shift_one, shift_two]...  9.57 us
    transpose x1, local copies, waits for them, and re-layouts, up_tables(): up_weight.reshape(2, 4, 2, 4, 8, channels, channels)  8.34 us
    ppermute x4, starting transfers between devices, extended_2(): lax.ppermute(tail, axis, [(i, (i + 1) % count) for i in range(ends)])  7.66 us
  transfers between devices with their start and end apart: 12, of which 4 were waited for; matrix products, arithmetic and copies ran while one was open for 8% of the time, Pallas kernels for 0%

profile of v2, /device:TPU:126, one launch (start us, length us, event | category | flops | bytes accessed | tf_op | source)
XLA Modules:
  0.0 144.3 jit_solution(12702495024084704602)
XLA Ops:
  0.0 8.3 %copy.7 = bf16[2,2,4,4,32,8,32]{6,5,4,3,2,1,0:T(8,128)(2,1)} copy(bf16[2,2,4,4,32,8,32]{6,4,5,3,1,2,0:T(8,128)(2,1)} %bitcast.110) | data formatting | bytes 2097152 | tf_op jit(solution)/shard_map/transpose | solution.py:37
  8.3 5.3 %reshape.208 = bf16[2,2,4,4,32,256]{5,4,3,2,1,0:T(8,128)(2,1)S(1)} reshape(bf16[2,2,4,4,32,8,32]{6,5,4,3,2,1,0:T(8,128)(2,1)} %copy.7) | data formatting | bytes 2097152 | tf_op jit(solution)/shard_map/reshape | solution.py:38
  14.8 2.0 %fusion.5 = bf16[2,2,4,4,128,512]{5,4,3,2,1,0:T(8,128)(2,1)S(1)} fusion(bf16[2,2,4,4,32,256]{5,4,3,2,1,0:T(8,128)(2,1)S(1)} %reshape.208, bf16[2,2,4,4,32,512]{5,4,3,2,1,0:T(8,128)(2,1)S(1)} %get-tuple-element.58, bf16[2,2,4,4,32,512]{5,4,3,2,1,0:T(8,128)(2,1)S(1)} %get-tuple-element.57), kind=kLoop, calls=%fused_computation.9 | loop fusion | flops 67108864 | bytes 13631488 | tf_op jit(solution)/shard_map/concatenate | solution.py:40
  18.1 1.7 %reshape.211 = f32[2,2,4,4,4,4,512]{6,5,4,3,2,1,0:T(4,128)} reshape(f32[64,16,512]{2,1,0:T(8,128)S(1)} %convolution_bitcast_fusion) | data formatting | bytes 4194304 | tf_op jit(solution)/shard_map/reshape | solution.py:76
  19.8 1.9 %slice_bitcast_fusion.3 = (f32[4,4,4,4,512]{4,3,2,1,0:T(4,128)S(1)}, f32[4,4,4,4,512]{4,3,2,1,0:T(4,128)S(1)}, f32[4,4,4,4,512]{4,3,2,1,0:T(4,128)S(1)}, f32[4,4,4,4,512]{4,3,2,1,0:T(4,128)S(1)}) fusion(f32[2,2,4,4,4,4,512]{6,5,4,3,2,1,0:T(4,128)} %reshape.211), kind=kLoop, calls=%fused_computation.79 | loop fusion | bytes 4194304 | tf_op jit(solution)/shard_map/squeeze | solution.py:81
  23.0 5.6 %collective-permute-start = (f32[2,20,512]{2,1,0:T(8,128)S(1)}, f32[2,20,512]{2,1,0:T(8,128)S(1)}, u32[]{:S(2)}, u32[]{:S(2)}) collective-permute-start(f32[2,20,512]{2,1,0:T(8,128)S(1)} %get-tuple-element.60), channel_id=1, source_target_pairs={{0,4},{4,8},{8,12},{12,16},{16,20},{20,24},{24,28},{28,32},{32,36}... | collective-permute-start | bytes 245768 | tf_op jit(solution)/shard_map/ppermute | solution.py:13
  28.6 1.9 %collective-permute-start.1 = (f32[2,20,512]{2,1,0:T(8,128)S(1)}, f32[2,20,512]{2,1,0:T(8,128)S(1)}, u32[]{:S(2)}, u32[]{:S(2)}) collective-permute-start(f32[2,20,512]{2,1,0:T(8,128)S(1)} %get-tuple-element.59), channel_id=1, source_target_pairs={{4,0},{8,4},{12,8},{16,12},{20,16},{24,20},{28,24},{32,28},{36,32}... | collective-permute-start | bytes 245768 | tf_op jit(solution)/shard_map/ppermute | solution.py:13
  31.0 9.9 %collective-permute-done.1 = f32[2,20,512]{2,1,0:T(8,128)S(1)} collective-permute-done((f32[2,20,512]{2,1,0:T(8,128)S(1)}, f32[2,20,512]{2,1,0:T(8,128)S(1)}, u32[]{:S(2)}, u32[]{:S(2)}) %collective-permute-start.1) | collective-permute-done | bytes 81952 | tf_op jit(solution)/shard_map/ppermute | solution.py:13
  41.0 1.9 %collective-permute-start.2 = (bf16[16,2,512]{2,1,0:T(2,128)(2,1)S(1)}, bf16[16,2,512]{2,1,0:T(2,128)(2,1)S(1)}, u32[]{:S(2)}, u32[]{:S(2)}) collective-permute-start(bf16[16,2,512]{2,1,0:T(2,128)(2,1)S(1)} %get-tuple-element.80), channel_id=1, source_target_pairs={{0,1},{1,2},{2,3},{4,5},{5,6},{6,7},{8,9},{9,10},{10,11},{12,13},{... | collective-permute-start | bytes 98312 | tf_op jit(solution)/shard_map/ppermute | solution.py:13
  43.7 3.6 %collective-permute-start.3 = (bf16[16,2,512]{2,1,0:T(2,128)(2,1)S(1)}, bf16[16,2,512]{2,1,0:T(2,128)(2,1)S(1)}, u32[]{:S(2)}, u32[]{:S(2)}) collective-permute-start(bf16[16,2,512]{2,1,0:T(2,128)(2,1)S(1)} %get-tuple-element.79), channel_id=1, source_target_pairs={{1,0},{2,1},{3,2},{5,4},{6,5},{7,6},{9,8},{10,9},{11,10},{13,12},{... | collective-permute-start | bytes 98312 | tf_op jit(solution)/shard_map/ppermute | solution.py:13
  49.2 1.9 %collective-permute-start.4 = (bf16[1,16,512]{2,1,0:T(8,128)(2,1)S(1)}, bf16[1,16,512]{2,1,0:T(8,128)(2,1)S(1)}, u32[]{:S(2)}, u32[]{:S(2)}) collective-permute-start(bf16[1,16,512]{2,1,0:T(8,128)(2,1)S(1)} %get-tuple-element.91), channel_id=1, source_target_pairs={{0,4},{4,8},{8,12},{12,16},{16,20},{20,24},{24,28},{28,32},{32,36}... | collective-permute-start | bytes 49160 | tf_op jit(solution)/shard_map/ppermute | solution.py:24
  51.1 4.1 %collective-permute-start.5 = (bf16[1,16,512]{2,1,0:T(8,128)(2,1)S(1)}, bf16[1,16,512]{2,1,0:T(8,128)(2,1)S(1)}, u32[]{:S(2)}, u32[]{:S(2)}) collective-permute-start(bf16[1,16,512]{2,1,0:T(8,128)(2,1)S(1)} %get-tuple-element.92), channel_id=1, source_target_pairs={{4,0},{8,4},{12,8},{16,12},{20,16},{24,20},{28,24},{32,28},{36,32}... | collective-permute-start | bytes 49160 | tf_op jit(solution)/shard_map/ppermute | solution.py:26
  55.7 6.9 %collective-permute-done.5 = bf16[1,16,512]{2,1,0:T(8,128)(2,1)S(1)} collective-permute-done((bf16[1,16,512]{2,1,0:T(8,128)(2,1)S(1)}, bf16[1,16,512]{2,1,0:T(8,128)(2,1)S(1)}, u32[]{:S(2)}, u32[]{:S(2)}) %collective-permute-start.5) | collective-permute-done | bytes 16416 | tf_op jit(solution)/shard_map/ppermute | solution.py:26
  63.3 1.9 %collective-permute-start.6 = (bf16[18,1,512]{2,1,0:T(2,128)(2,1)}, bf16[18,1,512]{2,1,0:T(2,128)(2,1)S(1)}, u32[]{:S(2)}, u32[]{:S(2)}) collective-permute-start(bf16[18,1,512]{2,1,0:T(2,128)(2,1)} %get-tuple-element.87), channel_id=1, source_target_pairs={{0,1},{1,2},{2,3},{4,5},{5,6},{6,7},{8,9},{9,10},{10,11},{12,13},{... | collective-permute-start | bytes 55304 | tf_op jit(solution)/shard_map/ppermute | solution.py:24
  65.2 3.6 %collective-permute-start.7 = (bf16[18,1,512]{2,1,0:T(2,128)(2,1)S(1)}, bf16[18,1,512]{2,1,0:T(2,128)(2,1)}, u32[]{:S(2)}, u32[]{:S(2)}) collective-permute-start(bf16[18,1,512]{2,1,0:T(2,128)(2,1)S(1)} %get-tuple-element.88), channel_id=1, source_target_pairs={{1,0},{2,1},{3,2},{5,4},{6,5},{7,6},{9,8},{10,9},{11,10},{13,12},{... | collective-permute-start | bytes 55304 | tf_op jit(solution)/shard_map/ppermute | solution.py:26
  70.1 1.9 %copy.9 = bf16[3,3,6,32,4,32]{5,4,3,2,1,0:T(4,128)(2,1)S(1)} copy(bf16[3,3,6,32,4,32]{5,3,2,1,0,4:T(8,128)(2,1)S(1)} %fusion.19) | data formatting | bytes 884736 | tf_op jit(solution)/shard_map/concatenate | solution.py:61
  72.0 1.6 %reshape.215 = bf16[3,3,192,128]{3,2,1,0:T(8,128)(2,1)} reshape(bf16[3,3,6,32,4,32]{5,4,3,2,1,0:T(4,128)(2,1)S(1)} %copy.9) | data formatting | bytes 884736 | tf_op jit(solution)/shard_map/reshape | solution.py:62
  75.9 3.4 %fusion.41 = (bf16[16,16,4,192]{3,2,1,0:T(4,128)(2,1)}, bf16[16,16,4,192]{3,2,1,0:T(4,128)(2,1)}, bf16[16,16,4,192]{3,2,1,0:T(4,128)(2,1)S(1)}, bf16[16,16,4,192...) fusion(bf16[18,18,4,192]{3,2,1,0:T(4,128)(2,1)S(1)} %fusion.30), kind=kLoop, calls=%fused_computation.130 | loop fusion | bytes 7077888 | tf_op jit(solution)/shard_map/slice | solution.py:100
  79.4 2.2 %reshape.214 = bf16[1024,192]{1,0:T(8,128)(2,1)} reshape(bf16[16,16,4,192]{3,2,1,0:T(4,128)(2,1)} %get-tuple-element.78) | data formatting | bytes 786432 | tf_op jit(solution)/shard_map/reshape | solution.py:102
  84.0 2.2 %reshape.218 = bf16[1024,192]{1,0:T(8,128)(2,1)} reshape(bf16[16,16,4,192]{3,2,1,0:T(4,128)(2,1)} %get-tuple-element.75) | data formatting | bytes 786432 | tf_op jit(solution)/shard_map/reshape | solution.py:102
  89.3 2.2 %reshape.223 = bf16[1024,192]{1,0:T(8,128)(2,1)} reshape(bf16[16,16,4,192]{3,2,1,0:T(4,128)(2,1)} %get-tuple-element.70) | data formatting | bytes 786432 | tf_op jit(solution)/shard_map/reshape | solution.py:102
  98.6 1.9 %collective-permute-start.8 = (bf16[1,16,512]{2,1,0:T(8,128)(2,1)S(1)}, bf16[1,16,512]{2,1,0:T(8,128)(2,1)S(1)}, u32[]{:S(2)}, u32[]{:S(2)}) collective-permute-start(bf16[1,16,512]{2,1,0:T(8,128)(2,1)S(1)} %get-tuple-element.89), channel_id=1, source_target_pairs={{0,4},{4,8},{8,12},{12,16},{16,20},{20,24},{24,28},{28,32},{32,36}... | collective-permute-start | bytes 49160 | tf_op jit(solution)/shard_map/ppermute | solution.py:24
  100.6 3.9 %collective-permute-start.9 = (bf16[1,16,512]{2,1,0:T(8,128)(2,1)S(1)}, bf16[1,16,512]{2,1,0:T(8,128)(2,1)S(1)}, u32[]{:S(2)}, u32[]{:S(2)}) collective-permute-start(bf16[1,16,512]{2,1,0:T(8,128)(2,1)S(1)} %get-tuple-element.90), channel_id=1, source_target_pairs={{4,0},{8,4},{12,8},{16,12},{20,16},{24,20},{28,24},{32,28},{36,32}... | collective-permute-start | bytes 49160 | tf_op jit(solution)/shard_map/ppermute | solution.py:26
  105.2 6.7 %collective-permute-done.9 = bf16[1,16,512]{2,1,0:T(8,128)(2,1)S(1)} collective-permute-done((bf16[1,16,512]{2,1,0:T(8,128)(2,1)S(1)}, bf16[1,16,512]{2,1,0:T(8,128)(2,1)S(1)}, u32[]{:S(2)}, u32[]{:S(2)}) %collective-permute-start.9) | collective-permute-done | bytes 16416 | tf_op jit(solution)/shard_map/ppermute | solution.py:26
  112.6 1.9 %collective-permute-start.10 = (bf16[18,1,512]{2,1,0:T(2,128)(2,1)}, bf16[18,1,512]{2,1,0:T(2,128)(2,1)S(1)}, u32[]{:S(2)}, u32[]{:S(2)}) collective-permute-start(bf16[18,1,512]{2,1,0:T(2,128)(2,1)} %get-tuple-element.85), channel_id=1, source_target_pairs={{0,1},{1,2},{2,3},{4,5},{5,6},{6,7},{8,9},{9,10},{10,11},{12,13},{... | collective-permute-start | bytes 55304 | tf_op jit(solution)/shard_map/ppermute | solution.py:24
  114.5 3.9 %collective-permute-start.11 = (bf16[18,1,512]{2,1,0:T(2,128)(2,1)S(1)}, bf16[18,1,512]{2,1,0:T(2,128)(2,1)}, u32[]{:S(2)}, u32[]{:S(2)}) collective-permute-start(bf16[18,1,512]{2,1,0:T(2,128)(2,1)S(1)} %get-tuple-element.86), channel_id=1, source_target_pairs={{1,0},{2,1},{3,2},{5,4},{6,5},{7,6},{9,8},{10,9},{11,10},{13,12},{... | collective-permute-start | bytes 55304 | tf_op jit(solution)/shard_map/ppermute | solution.py:26
  118.9 1.9 %copy.10 = bf16[3,3,6,32,4,32]{5,4,3,2,1,0:T(4,128)(2,1)S(1)} copy(bf16[3,3,6,32,4,32]{5,3,2,1,0,4:T(8,128)(2,1)S(1)} %fusion.23) | data formatting | bytes 884736 | tf_op jit(solution)/shard_map/concatenate | solution.py:61
  120.8 1.6 %reshape.227 = bf16[3,3,192,128]{3,2,1,0:T(8,128)(2,1)} reshape(bf16[3,3,6,32,4,32]{5,4,3,2,1,0:T(4,128)(2,1)S(1)} %copy.10) | data formatting | bytes 884736 | tf_op jit(solution)/shard_map/reshape | solution.py:62
  124.7 3.5 %fusion.40 = (bf16[16,16,4,192]{3,2,1,0:T(4,128)(2,1)}, bf16[16,16,4,192]{3,2,1,0:T(4,128)(2,1)S(1)}, bf16[16,16,4,192]{3,2,1,0:T(4,128)(2,1)S(1)}, bf16[16,16,4...) fusion(bf16[18,18,4,192]{3,2,1,0:T(4,128)(2,1)S(1)} %fusion.31), kind=kLoop, calls=%fused_computation.129 | loop fusion | bytes 7077888 | tf_op jit(solution)/shard_map/slice | solution.py:100
  128.2 2.2 %reshape.226 = bf16[1024,192]{1,0:T(8,128)(2,1)} reshape(bf16[16,16,4,192]{3,2,1,0:T(4,128)(2,1)} %get-tuple-element.69) | data formatting | bytes 786432 | tf_op jit(solution)/shard_map/reshape | solution.py:102
  130.3 2.2 %reshape.228 = bf16[1024,192]{1,0:T(8,128)(2,1)} reshape(bf16[16,16,4,192]{3,2,1,0:T(4,128)(2,1)} %get-tuple-element.68) | data formatting | bytes 786432 | tf_op jit(solution)/shard_map/reshape | solution.py:102
  132.5 2.2 %reshape.229 = bf16[1024,192]{1,0:T(8,128)(2,1)} reshape(bf16[16,16,4,192]{3,2,1,0:T(4,128)(2,1)} %get-tuple-element.67) | data formatting | bytes 786432 | tf_op jit(solution)/shard_map/reshape | solution.py:102
  (104 shorter events, 37.6 us)
Async XLA Ops:
  0.0 16.9 %copy-start = (bf16[4,4,128]{2,1,0:T(4,128)(2,1)S(1)}, bf16[4,4,128]{2,1,0:T(4,128)(2,1)}, u32[]{:S(2)}) copy-start(bf16[4,4,128]{2,1,0:T(4,128)(2,1)} %param.12) | copy-start | bytes 12292
  22.7 7.9 %copy-start.11 = (bf16[3,3,3,32,32]{4,3,2,1,0:T(8,128)(2,1)S(1)}, bf16[3,3,3,32,32]{4,3,2,1,0:T(8,128)(2,1)}, u32[]{:S(2)}) copy-start(bf16[3,3,3,32,32]{4,3,2,1,0:T(8,128)(2,1)} %param.14) | copy-start | bytes 165892
  23.0 7.9 %collective-permute-start = (f32[2,20,512]{2,1,0:T(8,128)S(1)}, f32[2,20,512]{2,1,0:T(8,128)S(1)}, u32[]{:S(2)}, u32[]{:S(2)}) collective-permute-start(f32[2,20,512]{2,1,0:T(8,128)S(1)} %get-tuple-element.60), channel_id=1, source_target_pairs={{0,4},{4,8},{8,12},{12,16},{16,20},{20,24},{24,28},{28,32},{32,36}... | collective-permute-start | bytes 245768 | tf_op jit(solution)/shard_map/ppermute | solution.py:13
  28.6 12.2 %collective-permute-start.1 = (f32[2,20,512]{2,1,0:T(8,128)S(1)}, f32[2,20,512]{2,1,0:T(8,128)S(1)}, u32[]{:S(2)}, u32[]{:S(2)}) collective-permute-start(f32[2,20,512]{2,1,0:T(8,128)S(1)} %get-tuple-element.59), channel_id=1, source_target_pairs={{4,0},{8,4},{12,8},{16,12},{20,16},{24,20},{28,24},{32,28},{36,32}... | collective-permute-start | bytes 245768 | tf_op jit(solution)/shard_map/ppermute | solution.py:13
  41.0 6.3 %collective-permute-start.2 = (bf16[16,2,512]{2,1,0:T(2,128)(2,1)S(1)}, bf16[16,2,512]{2,1,0:T(2,128)(2,1)S(1)}, u32[]{:S(2)}, u32[]{:S(2)}) collective-permute-start(bf16[16,2,512]{2,1,0:T(2,128)(2,1)S(1)} %get-tuple-element.80), channel_id=1, source_target_pairs={{0,1},{1,2},{2,3},{4,5},{5,6},{6,7},{8,9},{9,10},{10,11},{12,13},{... | collective-permute-start | bytes 98312 | tf_op jit(solution)/shard_map/ppermute | solution.py:13
  43.7 5.2 %collective-permute-start.3 = (bf16[16,2,512]{2,1,0:T(2,128)(2,1)S(1)}, bf16[16,2,512]{2,1,0:T(2,128)(2,1)S(1)}, u32[]{:S(2)}, u32[]{:S(2)}) collective-permute-start(bf16[16,2,512]{2,1,0:T(2,128)(2,1)S(1)} %get-tuple-element.79), channel_id=1, source_target_pairs={{1,0},{2,1},{3,2},{5,4},{6,5},{7,6},{9,8},{10,9},{11,10},{13,12},{... | collective-permute-start | bytes 98312 | tf_op jit(solution)/shard_map/ppermute | solution.py:13
  49.2 6.5 %collective-permute-start.4 = (bf16[1,16,512]{2,1,0:T(8,128)(2,1)S(1)}, bf16[1,16,512]{2,1,0:T(8,128)(2,1)S(1)}, u32[]{:S(2)}, u32[]{:S(2)}) collective-permute-start(bf16[1,16,512]{2,1,0:T(8,128)(2,1)S(1)} %get-tuple-element.91), channel_id=1, source_target_pairs={{0,4},{4,8},{8,12},{12,16},{16,20},{20,24},{24,28},{28,32},{32,36}... | collective-permute-start | bytes 49160 | tf_op jit(solution)/shard_map/ppermute | solution.py:24
  51.1 17.7 %copy-start.12 = (bf16[3,3,3,32,32]{4,3,2,1,0:T(8,128)(2,1)S(1)}, bf16[3,3,3,32,32]{4,3,2,1,0:T(8,128)(2,1)}, u32[]{:S(2)}) copy-start(bf16[3,3,3,32,32]{4,3,2,1,0:T(8,128)(2,1)} %param.15) | copy-start | bytes 165892
  51.1 11.5 %collective-permute-start.5 = (bf16[1,16,512]{2,1,0:T(8,128)(2,1)S(1)}, bf16[1,16,512]{2,1,0:T(8,128)(2,1)S(1)}, u32[]{:S(2)}, u32[]{:S(2)}) collective-permute-start(bf16[1,16,512]{2,1,0:T(8,128)(2,1)S(1)} %get-tuple-element.92), channel_id=1, source_target_pairs={{4,0},{8,4},{12,8},{16,12},{20,16},{24,20},{28,24},{32,28},{36,32}... | collective-permute-start | bytes 49160 | tf_op jit(solution)/shard_map/ppermute | solution.py:26
  63.3 10.4 %collective-permute-start.6 = (bf16[18,1,512]{2,1,0:T(2,128)(2,1)}, bf16[18,1,512]{2,1,0:T(2,128)(2,1)S(1)}, u32[]{:S(2)}, u32[]{:S(2)}) collective-permute-start(bf16[18,1,512]{2,1,0:T(2,128)(2,1)} %get-tuple-element.87), channel_id=1, source_target_pairs={{0,1},{1,2},{2,3},{4,5},{5,6},{6,7},{8,9},{9,10},{10,11},{12,13},{... | collective-permute-start | bytes 55304 | tf_op jit(solution)/shard_map/ppermute | solution.py:24
  65.2 8.4 %collective-permute-start.7 = (bf16[18,1,512]{2,1,0:T(2,128)(2,1)S(1)}, bf16[18,1,512]{2,1,0:T(2,128)(2,1)}, u32[]{:S(2)}, u32[]{:S(2)}) collective-permute-start(bf16[18,1,512]{2,1,0:T(2,128)(2,1)S(1)} %get-tuple-element.88), channel_id=1, source_target_pairs={{1,0},{2,1},{3,2},{5,4},{6,5},{7,6},{9,8},{10,9},{11,10},{13,12},{... | collective-permute-start | bytes 55304 | tf_op jit(solution)/shard_map/ppermute | solution.py:26
  91.5 2.8 %copy-start.9 = (bf16[3,3,192,128]{3,2,1,0:T(8,128)(2,1)S(1)}, bf16[3,3,192,128]{3,2,1,0:T(8,128)(2,1)}, u32[]{:S(2)}) copy-start(bf16[3,3,192,128]{3,2,1,0:T(8,128)(2,1)} %reshape.215) | copy-start | bytes 1327108
  91.5 3.1 %copy-start.6 = (bf16[1024,192]{1,0:T(8,128)(2,1)S(1)}, bf16[1024,192]{1,0:T(8,128)(2,1)}, u32[]{:S(2)}) copy-start(bf16[1024,192]{1,0:T(8,128)(2,1)} %reshape.218) | copy-start | bytes 1179652
  92.9 2.0 %copy-start.5 = (bf16[1024,192]{1,0:T(8,128)(2,1)S(1)}, bf16[1024,192]{1,0:T(8,128)(2,1)}, u32[]{:S(2)}) copy-start(bf16[1024,192]{1,0:T(8,128)(2,1)} %reshape.219) | copy-start | bytes 1179652
  95.2 1.0 copy-start.4
  96.3 8.2 %copy-start.2 = (bf16[3,3,6,32,1,32]{5,3,2,1,0,4:T(8,128)(2,1)S(1)}, bf16[3,3,6,32,1,32]{5,3,2,1,0,4:T(8,128)(2,1)}, u32[]{:S(2)}) copy-start(bf16[3,3,6,32,1,32]{5,3,2,1,0,4:T(8,128)(2,1)} %get-tuple-element.95) | copy-start | bytes 331780
  96.3 8.2 %copy-start.3 = (bf16[3,3,6,32,1,32]{5,3,2,1,0,4:T(8,128)(2,1)S(1)}, bf16[3,3,6,32,1,32]{5,3,2,1,0,4:T(8,128)(2,1)}, u32[]{:S(2)}) copy-start(bf16[3,3,6,32,1,32]{5,3,2,1,0,4:T(8,128)(2,1)} %get-tuple-element.96) | copy-start | bytes 331780
  98.6 6.6 %collective-permute-start.8 = (bf16[1,16,512]{2,1,0:T(8,128)(2,1)S(1)}, bf16[1,16,512]{2,1,0:T(8,128)(2,1)S(1)}, u32[]{:S(2)}, u32[]{:S(2)}) collective-permute-start(bf16[1,16,512]{2,1,0:T(8,128)(2,1)S(1)} %get-tuple-element.89), channel_id=1, source_target_pairs={{0,4},{4,8},{8,12},{12,16},{16,20},{20,24},{24,28},{28,32},{32,36}... | collective-permute-start | bytes 49160 | tf_op jit(solution)/shard_map/ppermute | solution.py:24
  100.6 11.4 %collective-permute-start.9 = (bf16[1,16,512]{2,1,0:T(8,128)(2,1)S(1)}, bf16[1,16,512]{2,1,0:T(8,128)(2,1)S(1)}, u32[]{:S(2)}, u32[]{:S(2)}) collective-permute-start(bf16[1,16,512]{2,1,0:T(8,128)(2,1)S(1)} %get-tuple-element.90), channel_id=1, source_target_pairs={{4,0},{8,4},{12,8},{16,12},{20,16},{24,20},{28,24},{32,28},{36,32}... | collective-permute-start | bytes 49160 | tf_op jit(solution)/shard_map/ppermute | solution.py:26
  112.6 9.8 %collective-permute-start.10 = (bf16[18,1,512]{2,1,0:T(2,128)(2,1)}, bf16[18,1,512]{2,1,0:T(2,128)(2,1)S(1)}, u32[]{:S(2)}, u32[]{:S(2)}) collective-permute-start(bf16[18,1,512]{2,1,0:T(2,128)(2,1)} %get-tuple-element.85), channel_id=1, source_target_pairs={{0,1},{1,2},{2,3},{4,5},{5,6},{6,7},{8,9},{9,10},{10,11},{12,13},{... | collective-permute-start | bytes 55304 | tf_op jit(solution)/shard_map/ppermute | solution.py:24
  114.5 7.9 %collective-permute-start.11 = (bf16[18,1,512]{2,1,0:T(2,128)(2,1)S(1)}, bf16[18,1,512]{2,1,0:T(2,128)(2,1)}, u32[]{:S(2)}, u32[]{:S(2)}) collective-permute-start(bf16[18,1,512]{2,1,0:T(2,128)(2,1)S(1)} %get-tuple-element.86), channel_id=1, source_target_pairs={{1,0},{2,1},{3,2},{5,4},{6,5},{7,6},{9,8},{10,9},{11,10},{13,12},{... | collective-permute-start | bytes 55304 | tf_op jit(solution)/shard_map/ppermute | solution.py:26
  138.4 2.8 %copy-start.8 = (bf16[1024,192]{1,0:T(8,128)(2,1)S(1)}, bf16[1024,192]{1,0:T(8,128)(2,1)}, u32[]{:S(2)}) copy-start(bf16[1024,192]{1,0:T(8,128)(2,1)} %reshape.229) | copy-start | bytes 1179652
  138.4 2.8 %copy-start.10 = (bf16[3,3,192,128]{3,2,1,0:T(8,128)(2,1)S(1)}, bf16[3,3,192,128]{3,2,1,0:T(8,128)(2,1)}, u32[]{:S(2)}) copy-start(bf16[3,3,192,128]{3,2,1,0:T(8,128)(2,1)} %reshape.227) | copy-start | bytes 1327108
  138.5 3.1 %copy-start.7 = (bf16[1024,192]{1,0:T(8,128)(2,1)S(1)}, bf16[1024,192]{1,0:T(8,128)(2,1)}, u32[]{:S(2)}) copy-start(bf16[1024,192]{1,0:T(8,128)(2,1)} %reshape.230) | copy-start | bytes 1179652
  142.7 1.5 %copy-start.1 = (bf16[4,4,128]{2,1,0:T(4,128)(2,1)S(1)}, bf16[4,4,128]{2,1,0:T(4,128)(2,1)}, u32[]{:S(2)}) copy-start(bf16[4,4,128]{2,1,0:T(4,128)(2,1)} %param.12) | copy-start | bytes 12292
